TPU v7x, 32 devices: a whole 2x2x4 slice. The times are simulated.
32 devices in a mesh: section: 4 (over y, x), coil: 2 (over core), space: 4 (over z).
Axes of the slice: x: 2, y: 2, z: 4, core: 2. Of those that a mesh axis runs over, the one named last changes fastest.
Arguments:
- image: float32 [4, 2, 2, 256, 256], P(None, None, 'coil', 'space'), may hold values from -6 to 6
- sens: bfloat16 [4, 2, 2, 256, 512], P('coil', None, None, 'space'), may hold values from -2 to 2
- adjoint: float32 [4, 2, 2, 256, 256], P(None, None, 'coil', 'space'), may hold values from -6 to 6
- mask_bits: int32 [2, 256, 9], replicated, may hold values from 0 to 1073741823, as said below
- step_size: float32 [4], P('section'), may hold values from 0.3 to 1
- conv1_w: bfloat16 [4, 32, 108], P('section'), may hold values from -0.625 to 0.625
- conv1_b: float32 [4, 32], P('section'), may hold values from -1 to 1
- conv2_w: bfloat16 [4, 32, 108], P('section'), may hold values from -0.125 to 0.125
Outputs:
- cascade_images: float32 [4, 4, 2, 2, 256, 256], P('section', None, None, 'coil', 'space')
Inputs may be any that keep to these rules, and one draw needn't show every extreme that they name: `mask_bits`: bit b of word w in row (p, ky) is 1 where k-space point (ky, 30 w + b) is sampled in phase p; bits for points at or beyond 256 are 0.
All inputs are finite; a program needn't handle non-finite values.
Results may differ from a plain program's by a relative error of at most 0.01.
Values may be sent and summed in bfloat16 or wider, within the bound.
No kernel may reach another device: no remote copies, remote signals or barrier semaphores. Data moves between devices by JAX's collectives and lax.ppermute only.
A program may use at most 128 MiB of HBM per device.

v0:
```python
import math
import jax
import jax.numpy as jnp
from jax import lax
from jax.sharding import PartitionSpec as P


def extended(cells, sides, width):
    for axis, dim in sides:
        count = lax.axis_size(axis)
        ends = count - 1
        head = lax.slice_in_dim(cells, 0, width, axis=dim)
        tail = lax.slice_in_dim(cells, cells.shape[dim] - width, cells.shape[dim], axis=dim)
        cells = jnp.concatenate(
            [
                lax.ppermute(tail, axis, [(i, (i + 1) % count) for i in range(ends)]),
                cells,
                lax.ppermute(head, axis, [((i + 1) % count, i) for i in range(ends)]),
            ],
            axis=dim,
        )
    return cells


def passed_along(value, axis, steps):
    count = lax.axis_size(axis)
    leading, last = (max(0, -steps), min(count, count - steps))
    return lax.ppermute(value, axis, [(source, source + steps) for source in range(leading, last)])


def dft_tables(length):
    index = jnp.arange(length, dtype=jnp.int32)
    product = index[:, None] * index[None, :] % length
    angle = product.astype(jnp.float32) * (2.0 * math.pi / length)
    scale = 1.0 / math.sqrt(length)
    return (
        (jnp.cos(angle) * scale).astype(jnp.bfloat16),
        (jnp.sin(angle) * scale).astype(jnp.bfloat16),
    )


def unpack_mask(mask_bits, length_z):
    column = jnp.arange(length_z, dtype=jnp.int32)
    word_count = mask_bits.shape[2]
    select = (column[:, None] // 30 == jnp.arange(word_count, dtype=jnp.int32)[None, :]).astype(
        jnp.int32
    )
    chosen = jnp.sum(mask_bits[:, :, None, :] * select[None, None], axis=3)
    return (jnp.right_shift(chosen, column % 30) & 1).astype(jnp.float32)


def mult_last(values, table):
    return jnp.einsum("...n,nk->...k", values, table, preferred_element_type=jnp.float32)


def mult_rows(values, table):
    return jnp.einsum("kn,...nz->...kz", table, values, preferred_element_type=jnp.float32)


def along_last(real_part, imag_part, cos_table, sin_table, direction):
    first = mult_last(real_part, cos_table) + direction * mult_last(imag_part, sin_table)
    second = mult_last(imag_part, cos_table) - direction * mult_last(real_part, sin_table)
    return (first, second)


def along_rows(real_part, imag_part, cos_table, sin_table, direction):
    first = mult_rows(real_part, cos_table) + direction * mult_rows(imag_part, sin_table)
    second = mult_rows(imag_part, cos_table) - direction * mult_rows(real_part, sin_table)
    return (first, second)


def correlate(source, weights):
    channels = source.shape[0]
    out_x = source.shape[1] - 2
    out_y = source.shape[2] - 2
    length_z = source.shape[3]
    padded = jnp.pad(source, ((0, 0), (0, 0), (0, 0), (1, 1)))
    result = jnp.zeros((weights.shape[0], out_x, out_y, length_z), jnp.float32)
    for offset_x in range(3):
        pieces = []
        for offset_y in range(3):
            for offset_z in range(3):
                pieces.append(
                    padded[
                        :,
                        offset_x : offset_x + out_x,
                        offset_y : offset_y + out_y,
                        offset_z : offset_z + length_z,
                    ]
                )
        patches = jnp.stack(pieces, axis=0).reshape(9 * channels, out_x, out_y, length_z)
        weight_block = weights[:, offset_x * 9 * channels : (offset_x + 1) * 9 * channels]
        result = result + jnp.einsum(
            "ok,kxyz->oxyz", weight_block, patches, preferred_element_type=jnp.float32
        )
    return result


def per_device(image, sens, adjoint, mask_bits, step_size, conv1_w, conv1_b, conv2_w):
    channels = image.shape[0]
    slab_count = image.shape[1]
    row_count = image.shape[3]
    length_z = image.shape[4]
    phases = mask_bits.shape[0]
    length_y = mask_bits.shape[1]
    planes = lax.axis_size("coil")
    spaces = lax.axis_size("space")
    coil_local = sens.shape[0]
    item_count = coil_local * planes * phases
    item_local = item_count // spaces
    hidden_width = conv1_w.shape[1]
    section_index = lax.axis_index("section")
    space_index = lax.axis_index("space")
    sampled = unpack_mask(mask_bits, length_z)
    cos_z, sin_z = dft_tables(length_z)
    cos_y, sin_y = dft_tables(length_y)
    step_rate = step_size[0]
    first_w = conv1_w[0]
    bias_one = conv1_b[0]
    second_w = (
        conv2_w[0]
        .reshape(hidden_width, 27, channels)
        .transpose(2, 1, 0)
        .reshape(channels, 27 * hidden_width)
    )
    item_ids = space_index * item_local + jnp.arange(item_local, dtype=jnp.int32)
    phase_pick = (
        item_ids[:, None] % phases == jnp.arange(phases, dtype=jnp.int32)[None, :]
    ).astype(jnp.float32)
    item_mask = jnp.einsum("kp,pyz->kyz", phase_pick, sampled)

    def cascade(current, slab_index):
        coil_maps = lax.dynamic_index_in_dim(sens, slab_index, 1, keepdims=False)
        coil_maps = coil_maps.reshape(coil_local, planes, row_count, 2, length_z)
        map_re = coil_maps[:, :, :, 0].astype(jnp.float32)[:, :, None]
        map_im = coil_maps[:, :, :, 1].astype(jnp.float32)[:, :, None]
        adjoint_slab = lax.dynamic_index_in_dim(adjoint, slab_index, 1, keepdims=False)
        gathered = lax.all_gather(current.astype(jnp.bfloat16), "coil", axis=1, tiled=True)
        planar = (
            gathered.reshape(phases, 2, planes, row_count, length_z)
            .transpose(2, 0, 1, 3, 4)
            .astype(jnp.float32)
        )
        image_re = planar[:, :, 0][None]
        image_im = planar[:, :, 1][None]
        coil_re = (map_re * image_re - map_im * image_im).astype(jnp.bfloat16)
        coil_im = (map_re * image_im + map_im * image_re).astype(jnp.bfloat16)
        coil_img = jnp.stack([coil_re, coil_im], axis=3).reshape(item_count, 2, row_count, length_z)
        exchanged = lax.all_to_all(coil_img, "space", split_axis=0, concat_axis=2, tiled=True)
        fwd_re, fwd_im = along_last(exchanged[:, 0], exchanged[:, 1], cos_z, sin_z, 1.0)
        spec_re, spec_im = along_rows(
            fwd_re.astype(jnp.bfloat16), fwd_im.astype(jnp.bfloat16), cos_y, sin_y, 1.0
        )
        spec_re = (spec_re * item_mask).astype(jnp.bfloat16)
        spec_im = (spec_im * item_mask).astype(jnp.bfloat16)
        inv_re, inv_im = along_rows(spec_re, spec_im, cos_y, sin_y, -1.0)
        out_re, out_im = along_last(
            inv_re.astype(jnp.bfloat16), inv_im.astype(jnp.bfloat16), cos_z, sin_z, -1.0
        )
        outgoing = jnp.stack([out_re.astype(jnp.bfloat16), out_im.astype(jnp.bfloat16)], axis=1)
        returned_img = lax.all_to_all(outgoing, "space", split_axis=2, concat_axis=0, tiled=True)
        returned_img = returned_img.reshape(
            coil_local, planes, phases, 2, row_count, length_z
        ).astype(jnp.float32)
        back_re = returned_img[:, :, :, 0]
        back_im = returned_img[:, :, :, 1]
        part_re = jnp.sum(map_re * back_re + map_im * back_im, axis=0)
        part_im = jnp.sum(map_re * back_im - map_im * back_re, axis=0)
        partial_value = (
            jnp.stack([part_re, part_im], axis=2)
            .transpose(1, 2, 0, 3, 4)
            .reshape(channels, planes, row_count, length_z)
        )
        shares = lax.psum_scatter(
            partial_value.astype(jnp.bfloat16), "coil", scatter_dimension=1, tiled=True
        ).astype(jnp.float32)
        updated = current - step_rate * (shares - adjoint_slab)
        lifted = updated.astype(jnp.bfloat16)
        widened = extended(lifted, (("coil", 1), ("space", 2)), 1)
        hidden = jnp.maximum(
            correlate(widened, first_w) + bias_one[:, None, None, None], 0.0
        ).astype(jnp.bfloat16)
        hidden_wide = extended(hidden, (("coil", 1), ("space", 2)), 1)
        return updated + correlate(hidden_wide, second_w)

    tick_count = slab_count + lax.axis_size("section") - 1

    def advance(tick_index, loop_state):
        incoming, outputs = loop_state
        offset = tick_index - section_index
        slab_index = jnp.clip(offset, 0, slab_count - 1)
        entering = lax.dynamic_index_in_dim(image, slab_index, 1, keepdims=False)
        current = jnp.where(section_index == 0, entering, incoming)
        finished = cascade(current, slab_index)
        active = (offset >= 0) & (offset < slab_count)
        previous = lax.dynamic_index_in_dim(outputs, slab_index, 1, keepdims=True)
        stored = jnp.where(active, finished[:, None], previous)
        outputs = lax.dynamic_update_slice_in_dim(outputs, stored, slab_index, 1)
        passed = passed_along(finished.astype(jnp.bfloat16), "section", 1).astype(finished.dtype)
        return (passed, outputs)

    initial = (jnp.zeros_like(image[:, 0]), jnp.zeros_like(image))
    last_in, outputs = lax.fori_loop(0, tick_count, advance, initial)
    return outputs[None]


def solution(mesh):
    in_specs = (
        P(None, None, "coil", "space", None),
        P("coil", None, None, "space", None),
        P(None, None, "coil", "space", None),
        P(),
        P("section"),
        P("section", None, None),
        P("section", None),
        P("section", None, None),
    )
    out_specs = P("section", None, None, "coil", "space", None)
    return jax.shard_map(
        per_device, mesh=mesh, in_specs=in_specs, out_specs=out_specs, check_vma=False
    )
```

profile of v0, /device:TPU:20, one launch (start us, length us, event | category | flops | bytes accessed | tf_op | source)
XLA Modules:
  0.0 1037.9 jit_solution(15423953089467877045)
XLA Ops:
  10.2 1020.9 %while.20 = (s32[]{:T(128)}, f32[4,1,64,256]{3,0,2,1:T(4,128)S(1)}, f32[4,2,1,64,256]{4,3,1,0,2:T(8,128)}, pred[]{:T(512)}, s32[]{:T(128)}, /*index=5*/f32[4,2,1...) while((s32[]{:T(128)}, f32[4,1,64,256]{3,0,2,1:T(4,128)S(1)}, ...), condition=%wide.region_5.6_spmd.clone.clone, body=%wide.region_1.5_spmd.clone.clone.sunk | while | flops 1387907712 | bytes 364505152 | solution.py:203
  15.4 17.1 %all_to_all.86 = bf16[8,2,64,256]{3,2,1,0:T(8,128)(2,1)S(1)} all-to-all(bf16[8,2,64,256]{3,2,1,0:T(8,128)(2,1)S(1)} %copy.304), channel_id=1, replica_groups=mesh['section'=4,'coil'=2,'space'=4] {'space'}, dimensions={0} | all-to-all | bytes 1048576 | tf_op jit(solution)/shard_map/while/body/eval_jaxpr/all_to_all | solution.py:149
  52.8 16.6 %all_to_all.87 = bf16[2,2,256,256]{3,0,1,2:T(2,128)(2,1)S(1)} all-to-all(bf16[2,2,256,256]{3,0,1,2:T(2,128)(2,1)S(1)} %copy.306), channel_id=1, replica_groups=mesh['section'=4,'coil'=2,'space'=4] {'space'}, dimensions={2} | all-to-all | bytes 1048576 | tf_op jit(solution)/shard_map/while/body/eval_jaxpr/all_to_all | solution.py:161
  143.8 13.3 %copy.313 = bf16[9,32,1,64,256]{4,3,1,0,2:T(8,128)(2,1)} copy(bf16[9,32,1,64,256]{4,1,3,2,0:T(8,128)(2,1)} %fusion.424) | data formatting | bytes 18874368 | tf_op jit(solution)/shard_map/while/body/eval_jaxpr/stack | solution.py:91
  157.1 13.5 %copy.314 = bf16[9,32,1,64,256]{4,3,1,0,2:T(8,128)(2,1)} copy(bf16[9,32,1,64,256]{4,1,3,2,0:T(8,128)(2,1)} %copy-done.1) | data formatting | bytes 18874368 | tf_op jit(solution)/shard_map/while/body/eval_jaxpr/stack | solution.py:91
  184.9 13.3 %copy.315 = bf16[9,32,1,64,256]{4,3,1,0,2:T(8,128)(2,1)} copy(bf16[9,32,1,64,256]{4,1,3,2,0:T(8,128)(2,1)} %copy-done) | data formatting | bytes 18874368 | tf_op jit(solution)/shard_map/while/body/eval_jaxpr/stack | solution.py:91
  220.3 17.0 %all_to_all.86 = bf16[8,2,64,256]{3,2,1,0:T(8,128)(2,1)S(1)} all-to-all(bf16[8,2,64,256]{3,2,1,0:T(8,128)(2,1)S(1)} %copy.304), channel_id=1, replica_groups=mesh['section'=4,'coil'=2,'space'=4] {'space'}, dimensions={0} | all-to-all | bytes 1048576 | tf_op jit(solution)/shard_map/while/body/eval_jaxpr/all_to_all | solution.py:149
  257.4 16.6 %all_to_all.87 = bf16[2,2,256,256]{3,0,1,2:T(2,128)(2,1)S(1)} all-to-all(bf16[2,2,256,256]{3,0,1,2:T(2,128)(2,1)S(1)} %copy.306), channel_id=1, replica_groups=mesh['section'=4,'coil'=2,'space'=4] {'space'}, dimensions={2} | all-to-all | bytes 1048576 | tf_op jit(solution)/shard_map/while/body/eval_jaxpr/all_to_all | solution.py:161
  347.6 13.3 %copy.313 = bf16[9,32,1,64,256]{4,3,1,0,2:T(8,128)(2,1)} copy(bf16[9,32,1,64,256]{4,1,3,2,0:T(8,128)(2,1)} %fusion.424) | data formatting | bytes 18874368 | tf_op jit(solution)/shard_map/while/body/eval_jaxpr/stack | solution.py:91
  360.9 13.5 %copy.314 = bf16[9,32,1,64,256]{4,3,1,0,2:T(8,128)(2,1)} copy(bf16[9,32,1,64,256]{4,1,3,2,0:T(8,128)(2,1)} %copy-done.1) | data formatting | bytes 18874368 | tf_op jit(solution)/shard_map/while/body/eval_jaxpr/stack | solution.py:91
  388.7 13.3 %copy.315 = bf16[9,32,1,64,256]{4,3,1,0,2:T(8,128)(2,1)} copy(bf16[9,32,1,64,256]{4,1,3,2,0:T(8,128)(2,1)} %copy-done) | data formatting | bytes 18874368 | tf_op jit(solution)/shard_map/while/body/eval_jaxpr/stack | solution.py:91
  424.1 17.0 %all_to_all.86 = bf16[8,2,64,256]{3,2,1,0:T(8,128)(2,1)S(1)} all-to-all(bf16[8,2,64,256]{3,2,1,0:T(8,128)(2,1)S(1)} %copy.304), channel_id=1, replica_groups=mesh['section'=4,'coil'=2,'space'=4] {'space'}, dimensions={0} | all-to-all | bytes 1048576 | tf_op jit(solution)/shard_map/while/body/eval_jaxpr/all_to_all | solution.py:149
  461.3 16.6 %all_to_all.87 = bf16[2,2,256,256]{3,0,1,2:T(2,128)(2,1)S(1)} all-to-all(bf16[2,2,256,256]{3,0,1,2:T(2,128)(2,1)S(1)} %copy.306), channel_id=1, replica_groups=mesh['section'=4,'coil'=2,'space'=4] {'space'}, dimensions={2} | all-to-all | bytes 1048576 | tf_op jit(solution)/shard_map/while/body/eval_jaxpr/all_to_all | solution.py:161
  551.4 13.3 %copy.313 = bf16[9,32,1,64,256]{4,3,1,0,2:T(8,128)(2,1)} copy(bf16[9,32,1,64,256]{4,1,3,2,0:T(8,128)(2,1)} %fusion.424) | data formatting | bytes 18874368 | tf_op jit(solution)/shard_map/while/body/eval_jaxpr/stack | solution.py:91
  564.7 13.5 %copy.314 = bf16[9,32,1,64,256]{4,3,1,0,2:T(8,128)(2,1)} copy(bf16[9,32,1,64,256]{4,1,3,2,0:T(8,128)(2,1)} %copy-done.1) | data formatting | bytes 18874368 | tf_op jit(solution)/shard_map/while/body/eval_jaxpr/stack | solution.py:91
  592.4 13.3 %copy.315 = bf16[9,32,1,64,256]{4,3,1,0,2:T(8,128)(2,1)} copy(bf16[9,32,1,64,256]{4,1,3,2,0:T(8,128)(2,1)} %copy-done) | data formatting | bytes 18874368 | tf_op jit(solution)/shard_map/while/body/eval_jaxpr/stack | solution.py:91
  627.9 17.0 %all_to_all.86 = bf16[8,2,64,256]{3,2,1,0:T(8,128)(2,1)S(1)} all-to-all(bf16[8,2,64,256]{3,2,1,0:T(8,128)(2,1)S(1)} %copy.304), channel_id=1, replica_groups=mesh['section'=4,'coil'=2,'space'=4] {'space'}, dimensions={0} | all-to-all | bytes 1048576 | tf_op jit(solution)/shard_map/while/body/eval_jaxpr/all_to_all | solution.py:149
  665.0 16.6 %all_to_all.87 = bf16[2,2,256,256]{3,0,1,2:T(2,128)(2,1)S(1)} all-to-all(bf16[2,2,256,256]{3,0,1,2:T(2,128)(2,1)S(1)} %copy.306), channel_id=1, replica_groups=mesh['section'=4,'coil'=2,'space'=4] {'space'}, dimensions={2} | all-to-all | bytes 1048576 | tf_op jit(solution)/shard_map/while/body/eval_jaxpr/all_to_all | solution.py:161
  755.2 13.3 %copy.313 = bf16[9,32,1,64,256]{4,3,1,0,2:T(8,128)(2,1)} copy(bf16[9,32,1,64,256]{4,1,3,2,0:T(8,128)(2,1)} %fusion.424) | data formatting | bytes 18874368 | tf_op jit(solution)/shard_map/while/body/eval_jaxpr/stack | solution.py:91
  768.5 13.5 %copy.314 = bf16[9,32,1,64,256]{4,3,1,0,2:T(8,128)(2,1)} copy(bf16[9,32,1,64,256]{4,1,3,2,0:T(8,128)(2,1)} %copy-done.1) | data formatting | bytes 18874368 | tf_op jit(solution)/shard_map/while/body/eval_jaxpr/stack | solution.py:91
  831.7 17.0 %all_to_all.86 = bf16[8,2,64,256]{3,2,1,0:T(8,128)(2,1)S(1)} all-to-all(bf16[8,2,64,256]{3,2,1,0:T(8,128)(2,1)S(1)} %copy.304), channel_id=1, replica_groups=mesh['section'=4,'coil'=2,'space'=4] {'space'}, dimensions={0} | all-to-all | bytes 1048576 | tf_op jit(solution)/shard_map/while/body/eval_jaxpr/all_to_all | solution.py:149
  868.8 16.6 %all_to_all.87 = bf16[2,2,256,256]{3,0,1,2:T(2,128)(2,1)S(1)} all-to-all(bf16[2,2,256,256]{3,0,1,2:T(2,128)(2,1)S(1)} %copy.306), channel_id=1, replica_groups=mesh['section'=4,'coil'=2,'space'=4] {'space'}, dimensions={2} | all-to-all | bytes 1048576 | tf_op jit(solution)/shard_map/while/body/eval_jaxpr/all_to_all | solution.py:161
  959.0 13.3 %copy.313 = bf16[9,32,1,64,256]{4,3,1,0,2:T(8,128)(2,1)} copy(bf16[9,32,1,64,256]{4,1,3,2,0:T(8,128)(2,1)} %fusion.424) | data formatting | bytes 18874368 | tf_op jit(solution)/shard_map/while/body/eval_jaxpr/stack | solution.py:91
  972.3 13.5 %copy.314 = bf16[9,32,1,64,256]{4,3,1,0,2:T(8,128)(2,1)} copy(bf16[9,32,1,64,256]{4,1,3,2,0:T(8,128)(2,1)} %copy-done.1) | data formatting | bytes 18874368 | tf_op jit(solution)/shard_map/while/body/eval_jaxpr/stack | solution.py:91
  (623 shorter events, 678.1 us)
Async XLA Ops:
  10.2 69.6 %reduce-scatter.2.cloned.1.call-start = ((), (), s32[]{:S(2)}) async-start(), calls=%async_computation.3 | async-start | bytes 393216 | tf_op jit(solution)/shard_map/while/body/eval_jaxpr/reduce_scatter | solution.py:174
  87.8 5.9 collective-permute-start.2
  109.6 6.2 collective-permute-start.6
  112.0 6.2 collective-permute-start.7
  207.1 7.8 collective-permute-start.8
  215.1 68.5 %reduce-scatter.2.cloned.1.call-start = ((), (), s32[]{:S(2)}) async-start(), calls=%async_computation.3 | async-start | bytes 393216 | tf_op jit(solution)/shard_map/while/body/eval_jaxpr/reduce_scatter | solution.py:174
  291.6 5.9 collective-permute-start.2
  313.4 6.2 collective-permute-start.6
  315.8 6.2 collective-permute-start.7
  410.9 7.8 collective-permute-start.8
  418.9 68.5 %reduce-scatter.2.cloned.1.call-start = ((), (), s32[]{:S(2)}) async-start(), calls=%async_computation.3 | async-start | bytes 393216 | tf_op jit(solution)/shard_map/while/body/eval_jaxpr/reduce_scatter | solution.py:174
  495.4 5.9 collective-permute-start.2
  517.1 6.2 collective-permute-start.6
  519.6 6.2 collective-permute-start.7
  614.6 7.8 collective-permute-start.8
  622.7 68.5 %reduce-scatter.2.cloned.1.call-start = ((), (), s32[]{:S(2)}) async-start(), calls=%async_computation.3 | async-start | bytes 393216 | tf_op jit(solution)/shard_map/while/body/eval_jaxpr/reduce_scatter | solution.py:174
  699.2 5.9 collective-permute-start.2
  720.9 6.2 collective-permute-start.6
  723.4 6.2 collective-permute-start.7
  818.4 7.8 collective-permute-start.8
  826.5 68.5 %reduce-scatter.2.cloned.1.call-start = ((), (), s32[]{:S(2)}) async-start(), calls=%async_computation.3 | async-start | bytes 393216 | tf_op jit(solution)/shard_map/while/body/eval_jaxpr/reduce_scatter | solution.py:174
  924.7 6.2 collective-permute-start.6
  927.2 6.2 collective-permute-start.7
  1022.2 7.8 collective-permute-start.8
  (74 other events, 691.7 us)
Sparse Core Ops, SparseCore 0:
  70.6 9.1 reduce-scatter.1
  275.2 8.3 reduce-scatter.1
  479.0 8.2 reduce-scatter.1
  682.8 8.2 reduce-scatter.1
  886.6 8.3 reduce-scatter.1
where the time goes:
time: 1040 us
  local copies, waits for them, and re-layouts  328 us (32%)
  matrix products  227 us (22%)
  blocking collectives  178 us (17%)
  starting transfers between devices  120 us (12%)
  waiting for transfers between devices  98.9 us (10%)
  other arithmetic  67.8 us (7%)
  between operations  13.4 us (1%)
    another operation x45, local copies, waits for them, and re-layouts, correlate(): jnp.stack(pieces, axis=0).reshape(9 * channels, out_x, out_y, length_z)  223 us
    dot_general x30, matrix products, correlate(): jnp.einsum('ok,kxyz->oxyz', weight_block, patches, preferred_element_type...  130 us
    all_to_all x5, blocking collectives, cascade(): lax.all_to_all(coil_img, 'space', split_axis=0, concat_axis=2, tiled=True)  85 us
    all_to_all x5, blocking collectives, cascade(): lax.all_to_all(outgoing, 'space', split_axis=2, concat_axis=0, tiled=True)  83 us
    while x175, local copies, waits for them, and re-layouts  79.3 us
    ppermute x20, starting transfers between devices, extended(): lax.ppermute(tail, axis, [(i, (i + 1) % count) for i in range(ends)])  64.8 us
    dot_general x40, matrix products, mult_rows(): jnp.einsum('kn,...nz->...kz', table, values, preferred_element_type=jnp.f...  49.7 us
    dot_general x40, matrix products, mult_last(): jnp.einsum('...n,nk->...k', values, table, preferred_element_type=jnp.flo...  47.3 us
  transfers between devices with their start and end apart: 50, of which 40 were waited for; matrix products, arithmetic and copies ran while one was open for 1% of the time, Pallas kernels for 0%

commit v1 on v0

--- a/solution.py
+++ b/solution.py
@@ -3,6 +3,29 @@
 import jax.numpy as jnp
 from jax import lax
 from jax.sharding import PartitionSpec as P
+
+
+def cut_along(value, dim, size):
+    dims = value.shape
+    blocks = value.reshape(*dims[:dim], size, dims[dim] // size, *dims[dim + 1 :])
+    return jnp.moveaxis(blocks, dim, 0)
+
+
+def laid_out(parts, dim):
+    shape = list(parts.shape[1:])
+    shape[dim] *= parts.shape[0]
+    return jnp.moveaxis(parts, 0, dim).reshape(shape)
+
+
+def exchange_in_pairs(x, axis, split_dim, concat_dim):
+    count, position = (lax.axis_size(axis), lax.axis_index(axis))
+    blocks = cut_along(x, split_dim, count)
+    outs = [blocks[position]]
+    for lap in range(1, count):
+        sent = blocks[position ^ lap]
+        outs.append(lax.ppermute(sent, axis, [(i, i ^ lap) for i in range(count)]))
+    blocks = jnp.stack(outs)[position ^ jnp.arange(count)]
+    return laid_out(blocks, concat_dim)
 
 
 def extended(cells, sides, width):
@@ -158,7 +181,7 @@
             inv_re.astype(jnp.bfloat16), inv_im.astype(jnp.bfloat16), cos_z, sin_z, -1.0
         )
         outgoing = jnp.stack([out_re.astype(jnp.bfloat16), out_im.astype(jnp.bfloat16)], axis=1)
-        returned_img = lax.all_to_all(outgoing, "space", split_axis=2, concat_axis=0, tiled=True)
+        returned_img = exchange_in_pairs(outgoing, "space", 2, 0)
         returned_img = returned_img.reshape(
             coil_local, planes, phases, 2, row_count, length_z
         ).astype(jnp.float32)

time: 1040 us -> 1030 us (level)
  blocking collectives: 178 us -> 9.97 us
  waiting for transfers between devices: 98.9 us -> 197 us
  starting transfers between devices: 120 us -> 170 us
    all_to_all x10 -> x0, blocking collectives: 168 us -> none  [the longest x5 85 us: cascade(): lax.all_to_all(coil_img, 'space', split_axis=0, concat_axis=2, tiled=True)]
    all_to_all x0 -> x5, waiting for transfers between devices: none -> 57.6 us  [cascade(): lax.all_to_all(coil_img, 'space', split_axis=0, concat_axis=2, tiled=True)]
    ppermute x0 -> x15, waiting for transfers between devices: none -> 39.6 us  [exchange_in_pairs(): outs.append(lax.ppermute(sent, axis, [(i, i ^ lap) for i in range(count)]))]
    all_to_all x0 -> x5, starting transfers between devices: none -> 25.7 us  [cascade(): lax.all_to_all(coil_img, 'space', split_axis=0, concat_axis=2, tiled=True)]
    ppermute x0 -> x15, starting transfers between devices: none -> 24.8 us  [exchange_in_pairs(): outs.append(lax.ppermute(sent, axis, [(i, i ^ lap) for i in range(count)]))]
  transfers between devices with their start and end apart: 50 -> 70, of which waited for: 40 -> 60; matrix products, arithmetic and copies ran while one was open for 1% -> 1% of each run, Pallas kernels for 0% -> 0%
where the time goes in v1:
time: 1030 us; the launch traced here: 1020 us
  local copies, waits for them, and re-layouts  328 us (32%)
  matrix products  227 us (22%)
  waiting for transfers between devices  197 us (19%)
  starting transfers between devices  170 us (17%)
  other arithmetic  72.7 us (7%)
  between operations  13.4 us (1%)
    another operation x45, local copies, waits for them, and re-layouts, correlate(): jnp.stack(pieces, axis=0).reshape(9 * channels, out_x, out_y, length_z)  223 us
    dot_general x30, matrix products, correlate(): jnp.einsum('ok,kxyz->oxyz', weight_block, patches, preferred_element_type...  130 us
    while x175, local copies, waits for them, and re-layouts  79.5 us
    ppermute x20, starting transfers between devices, extended(): lax.ppermute(tail, axis, [(i, (i + 1) % count) for i in range(ends)])  64.9 us
    all_to_all x5, waiting for transfers between devices, cascade(): lax.all_to_all(coil_img, 'space', split_axis=0, concat_axis=2, tiled=True)  57.6 us
    dot_general x40, matrix products, mult_rows(): jnp.einsum('kn,...nz->...kz', table, values, preferred_element_type=jnp.f...  49.7 us
    dot_general x40, matrix products, mult_last(): jnp.einsum('...n,nk->...k', values, table, preferred_element_type=jnp.flo...  47.4 us
    ppermute x15, waiting for transfers between devices, exchange_in_pairs(): outs.append(lax.ppermute(sent, axis, [(i, i ^ lap) for i in range(count)]))  39.6 us
  transfers between devices with their start and end apart: 70, of which 60 were waited for; matrix products, arithmetic and copies ran while one was open for 1% of the time, Pallas kernels for 0%

profile of v1, /device:TPU:20, one launch (start us, length us, event | category | flops | bytes accessed | tf_op | source)
XLA Modules:
  0.0 1023.4 jit_solution(10854624182477121311)
XLA Ops:
  10.2 1006.4 %while.20 = (s32[]{:T(128)}, f32[4,1,64,256]{3,0,2,1:T(4,128)S(1)}, f32[4,2,1,64,256]{4,3,1,0,2:T(8,128)}, pred[]{:T(512)}, s32[]{:T(128)}, /*index=5*/f32[4,2,1...) while((s32[]{:T(128)}, f32[4,1,64,256]{3,0,2,1:T(4,128)S(1)}, ...), condition=%wide.region_5.6_spmd.clone.clone, body=%wide.region_1.5_spmd.clone.clone.sunk | while | flops 1388957312 | bytes 366606848 | solution.py:226
  21.3 11.5 %all-to-all-done = bf16[8,2,64,256]{3,2,1,0:T(8,128)(2,1)S(1)} async-done(((bf16[8,2,64,256]{3,2,1,0:T(8,128)(2,1)}), bf16[8,2,64,256]{3,2,1,0:T(8,128)(2,1)S(1)}, u32[]{:S(2)}, u32[]{:S(2)}) %all-to-all-start) | async-done | bytes 524320 | tf_op jit(solution)/shard_map/while/body/eval_jaxpr/all_to_all | solution.py:172
  140.9 13.2 %copy.333 = bf16[9,32,1,64,256]{4,3,1,0,2:T(8,128)(2,1)} copy(bf16[9,32,1,64,256]{4,1,3,2,0:T(8,128)(2,1)} %fusion.431) | data formatting | bytes 18874368 | tf_op jit(solution)/shard_map/while/body/eval_jaxpr/stack | solution.py:114
  154.2 13.5 %copy.334 = bf16[9,32,1,64,256]{4,3,1,0,2:T(8,128)(2,1)} copy(bf16[9,32,1,64,256]{4,1,3,2,0:T(8,128)(2,1)} %copy-done.1) | data formatting | bytes 18874368 | tf_op jit(solution)/shard_map/while/body/eval_jaxpr/stack | solution.py:114
  181.9 13.3 %copy.335 = bf16[9,32,1,64,256]{4,3,1,0,2:T(8,128)(2,1)} copy(bf16[9,32,1,64,256]{4,1,3,2,0:T(8,128)(2,1)} %copy-done) | data formatting | bytes 18874368 | tf_op jit(solution)/shard_map/while/body/eval_jaxpr/stack | solution.py:114
  195.2 8.9 fusion.434
  223.3 11.5 %all-to-all-done = bf16[8,2,64,256]{3,2,1,0:T(8,128)(2,1)S(1)} async-done(((bf16[8,2,64,256]{3,2,1,0:T(8,128)(2,1)}), bf16[8,2,64,256]{3,2,1,0:T(8,128)(2,1)S(1)}, u32[]{:S(2)}, u32[]{:S(2)}) %all-to-all-start) | async-done | bytes 524320 | tf_op jit(solution)/shard_map/while/body/eval_jaxpr/all_to_all | solution.py:172
  341.8 13.2 %copy.333 = bf16[9,32,1,64,256]{4,3,1,0,2:T(8,128)(2,1)} copy(bf16[9,32,1,64,256]{4,1,3,2,0:T(8,128)(2,1)} %fusion.431) | data formatting | bytes 18874368 | tf_op jit(solution)/shard_map/while/body/eval_jaxpr/stack | solution.py:114
  355.1 13.5 %copy.334 = bf16[9,32,1,64,256]{4,3,1,0,2:T(8,128)(2,1)} copy(bf16[9,32,1,64,256]{4,1,3,2,0:T(8,128)(2,1)} %copy-done.1) | data formatting | bytes 18874368 | tf_op jit(solution)/shard_map/while/body/eval_jaxpr/stack | solution.py:114
  382.8 13.3 %copy.335 = bf16[9,32,1,64,256]{4,3,1,0,2:T(8,128)(2,1)} copy(bf16[9,32,1,64,256]{4,1,3,2,0:T(8,128)(2,1)} %copy-done) | data formatting | bytes 18874368 | tf_op jit(solution)/shard_map/while/body/eval_jaxpr/stack | solution.py:114
  396.1 8.9 fusion.434
  424.2 11.5 %all-to-all-done = bf16[8,2,64,256]{3,2,1,0:T(8,128)(2,1)S(1)} async-done(((bf16[8,2,64,256]{3,2,1,0:T(8,128)(2,1)}), bf16[8,2,64,256]{3,2,1,0:T(8,128)(2,1)S(1)}, u32[]{:S(2)}, u32[]{:S(2)}) %all-to-all-start) | async-done | bytes 524320 | tf_op jit(solution)/shard_map/while/body/eval_jaxpr/all_to_all | solution.py:172
  542.7 13.2 %copy.333 = bf16[9,32,1,64,256]{4,3,1,0,2:T(8,128)(2,1)} copy(bf16[9,32,1,64,256]{4,1,3,2,0:T(8,128)(2,1)} %fusion.431) | data formatting | bytes 18874368 | tf_op jit(solution)/shard_map/while/body/eval_jaxpr/stack | solution.py:114
  555.9 13.5 %copy.334 = bf16[9,32,1,64,256]{4,3,1,0,2:T(8,128)(2,1)} copy(bf16[9,32,1,64,256]{4,1,3,2,0:T(8,128)(2,1)} %copy-done.1) | data formatting | bytes 18874368 | tf_op jit(solution)/shard_map/while/body/eval_jaxpr/stack | solution.py:114
  583.7 13.3 %copy.335 = bf16[9,32,1,64,256]{4,3,1,0,2:T(8,128)(2,1)} copy(bf16[9,32,1,64,256]{4,1,3,2,0:T(8,128)(2,1)} %copy-done) | data formatting | bytes 18874368 | tf_op jit(solution)/shard_map/while/body/eval_jaxpr/stack | solution.py:114
  597.0 8.9 fusion.434
  625.1 11.5 %all-to-all-done = bf16[8,2,64,256]{3,2,1,0:T(8,128)(2,1)S(1)} async-done(((bf16[8,2,64,256]{3,2,1,0:T(8,128)(2,1)}), bf16[8,2,64,256]{3,2,1,0:T(8,128)(2,1)S(1)}, u32[]{:S(2)}, u32[]{:S(2)}) %all-to-all-start) | async-done | bytes 524320 | tf_op jit(solution)/shard_map/while/body/eval_jaxpr/all_to_all | solution.py:172
  743.6 13.2 %copy.333 = bf16[9,32,1,64,256]{4,3,1,0,2:T(8,128)(2,1)} copy(bf16[9,32,1,64,256]{4,1,3,2,0:T(8,128)(2,1)} %fusion.431) | data formatting | bytes 18874368 | tf_op jit(solution)/shard_map/while/body/eval_jaxpr/stack | solution.py:114
  756.8 13.5 %copy.334 = bf16[9,32,1,64,256]{4,3,1,0,2:T(8,128)(2,1)} copy(bf16[9,32,1,64,256]{4,1,3,2,0:T(8,128)(2,1)} %copy-done.1) | data formatting | bytes 18874368 | tf_op jit(solution)/shard_map/while/body/eval_jaxpr/stack | solution.py:114
  784.6 13.3 %copy.335 = bf16[9,32,1,64,256]{4,3,1,0,2:T(8,128)(2,1)} copy(bf16[9,32,1,64,256]{4,1,3,2,0:T(8,128)(2,1)} %copy-done) | data formatting | bytes 18874368 | tf_op jit(solution)/shard_map/while/body/eval_jaxpr/stack | solution.py:114
  826.0 11.5 %all-to-all-done = bf16[8,2,64,256]{3,2,1,0:T(8,128)(2,1)S(1)} async-done(((bf16[8,2,64,256]{3,2,1,0:T(8,128)(2,1)}), bf16[8,2,64,256]{3,2,1,0:T(8,128)(2,1)S(1)}, u32[]{:S(2)}, u32[]{:S(2)}) %all-to-all-start) | async-done | bytes 524320 | tf_op jit(solution)/shard_map/while/body/eval_jaxpr/all_to_all | solution.py:172
  944.4 13.2 %copy.333 = bf16[9,32,1,64,256]{4,3,1,0,2:T(8,128)(2,1)} copy(bf16[9,32,1,64,256]{4,1,3,2,0:T(8,128)(2,1)} %fusion.431) | data formatting | bytes 18874368 | tf_op jit(solution)/shard_map/while/body/eval_jaxpr/stack | solution.py:114
  957.7 13.5 %copy.334 = bf16[9,32,1,64,256]{4,3,1,0,2:T(8,128)(2,1)} copy(bf16[9,32,1,64,256]{4,1,3,2,0:T(8,128)(2,1)} %copy-done.1) | data formatting | bytes 18874368 | tf_op jit(solution)/shard_map/while/body/eval_jaxpr/stack | solution.py:114
  985.4 13.3 %copy.335 = bf16[9,32,1,64,256]{4,3,1,0,2:T(8,128)(2,1)} copy(bf16[9,32,1,64,256]{4,1,3,2,0:T(8,128)(2,1)} %copy-done) | data formatting | bytes 18874368 | tf_op jit(solution)/shard_map/while/body/eval_jaxpr/stack | solution.py:114
  (683 shorter events, 720.5 us)
Async XLA Ops:
  16.1 16.7 %all-to-all-start = ((bf16[8,2,64,256]{3,2,1,0:T(8,128)(2,1)}), bf16[8,2,64,256]{3,2,1,0:T(8,128)(2,1)S(1)}, u32[]{:S(2)}, u32[]{:S(2)}) async-start(bf16[8,2,64,256]{3,2,1,0:T(8,128)(2,1)} %pad_maximum_fusion.24), calls=%async_computation | async-start | bytes 1048576 | tf_op jit(solution)/shard_map/while/body/eval_jaxpr/all_to_all | solution.py:172
  21.3 55.5 %reduce-scatter.2.cloned.1.call-start = ((), (), s32[]{:S(2)}) async-start(), calls=%async_computation.2 | async-start | bytes 393216 | tf_op jit(solution)/shard_map/while/body/eval_jaxpr/reduce_scatter | solution.py:197
  52.7 10.5 %collective-permute-start = (bf16[2,2,64,256]{3,2,1,0:T(8,128)(2,1)S(1)}, bf16[2,2,64,256]{3,2,1,0:T(8,128)(2,1)S(1)}, u32[]{:S(2)}, u32[]{:S(2)}) collective-permute-start(bf16[2,2,64,256]{3,2,1,0:T(8,128)(2,1)S(1)} %bitcast.629), channel_id=1, source_target_pairs={{0,3},{1,2},{2,1},{3,0},{4,7},{5,6},{6,5},{7,4},{8,11},{9,10},{10,... | collective-permute-start | bytes 393224 | tf_op jit(solution)/shard_map/while/body/eval_jaxpr/ppermute | solution.py:26
  53.4 11.2 %collective-permute-start.1 = (bf16[2,2,64,256]{3,2,1,0:T(8,128)(2,1)S(1)}, bf16[2,2,64,256]{3,2,1,0:T(8,128)(2,1)S(1)}, u32[]{:S(2)}, u32[]{:S(2)}) collective-permute-start(bf16[2,2,64,256]{3,2,1,0:T(8,128)(2,1)S(1)} %bitcast.630), channel_id=1, source_target_pairs={{0,2},{1,3},{2,0},{3,1},{4,6},{5,7},{6,4},{7,5},{8,10},{9,11},{10,... | collective-permute-start | bytes 393224 | tf_op jit(solution)/shard_map/while/body/eval_jaxpr/ppermute | solution.py:26
  57.6 8.1 collective-permute-start.2
  218.2 16.6 %all-to-all-start = ((bf16[8,2,64,256]{3,2,1,0:T(8,128)(2,1)}), bf16[8,2,64,256]{3,2,1,0:T(8,128)(2,1)S(1)}, u32[]{:S(2)}, u32[]{:S(2)}) async-start(bf16[8,2,64,256]{3,2,1,0:T(8,128)(2,1)} %pad_maximum_fusion.24), calls=%async_computation | async-start | bytes 1048576 | tf_op jit(solution)/shard_map/while/body/eval_jaxpr/all_to_all | solution.py:172
  223.3 54.4 %reduce-scatter.2.cloned.1.call-start = ((), (), s32[]{:S(2)}) async-start(), calls=%async_computation.2 | async-start | bytes 393216 | tf_op jit(solution)/shard_map/while/body/eval_jaxpr/reduce_scatter | solution.py:197
  254.4 10.4 %collective-permute-start = (bf16[2,2,64,256]{3,2,1,0:T(8,128)(2,1)S(1)}, bf16[2,2,64,256]{3,2,1,0:T(8,128)(2,1)S(1)}, u32[]{:S(2)}, u32[]{:S(2)}) collective-permute-start(bf16[2,2,64,256]{3,2,1,0:T(8,128)(2,1)S(1)} %bitcast.629), channel_id=1, source_target_pairs={{0,3},{1,2},{2,1},{3,0},{4,7},{5,6},{6,5},{7,4},{8,11},{9,10},{10,... | collective-permute-start | bytes 393224 | tf_op jit(solution)/shard_map/while/body/eval_jaxpr/ppermute | solution.py:26
  255.1 11.2 %collective-permute-start.1 = (bf16[2,2,64,256]{3,2,1,0:T(8,128)(2,1)S(1)}, bf16[2,2,64,256]{3,2,1,0:T(8,128)(2,1)S(1)}, u32[]{:S(2)}, u32[]{:S(2)}) collective-permute-start(bf16[2,2,64,256]{3,2,1,0:T(8,128)(2,1)S(1)} %bitcast.630), channel_id=1, source_target_pairs={{0,2},{1,3},{2,0},{3,1},{4,6},{5,7},{6,4},{7,5},{8,10},{9,11},{10,... | collective-permute-start | bytes 393224 | tf_op jit(solution)/shard_map/while/body/eval_jaxpr/ppermute | solution.py:26
  259.3 8.0 collective-permute-start.2
  419.1 16.6 %all-to-all-start = ((bf16[8,2,64,256]{3,2,1,0:T(8,128)(2,1)}), bf16[8,2,64,256]{3,2,1,0:T(8,128)(2,1)S(1)}, u32[]{:S(2)}, u32[]{:S(2)}) async-start(bf16[8,2,64,256]{3,2,1,0:T(8,128)(2,1)} %pad_maximum_fusion.24), calls=%async_computation | async-start | bytes 1048576 | tf_op jit(solution)/shard_map/while/body/eval_jaxpr/all_to_all | solution.py:172
  424.2 54.4 %reduce-scatter.2.cloned.1.call-start = ((), (), s32[]{:S(2)}) async-start(), calls=%async_computation.2 | async-start | bytes 393216 | tf_op jit(solution)/shard_map/while/body/eval_jaxpr/reduce_scatter | solution.py:197
  455.3 10.5 %collective-permute-start = (bf16[2,2,64,256]{3,2,1,0:T(8,128)(2,1)S(1)}, bf16[2,2,64,256]{3,2,1,0:T(8,128)(2,1)S(1)}, u32[]{:S(2)}, u32[]{:S(2)}) collective-permute-start(bf16[2,2,64,256]{3,2,1,0:T(8,128)(2,1)S(1)} %bitcast.629), channel_id=1, source_target_pairs={{0,3},{1,2},{2,1},{3,0},{4,7},{5,6},{6,5},{7,4},{8,11},{9,10},{10,... | collective-permute-start | bytes 393224 | tf_op jit(solution)/shard_map/while/body/eval_jaxpr/ppermute | solution.py:26
  456.0 11.2 %collective-permute-start.1 = (bf16[2,2,64,256]{3,2,1,0:T(8,128)(2,1)S(1)}, bf16[2,2,64,256]{3,2,1,0:T(8,128)(2,1)S(1)}, u32[]{:S(2)}, u32[]{:S(2)}) collective-permute-start(bf16[2,2,64,256]{3,2,1,0:T(8,128)(2,1)S(1)} %bitcast.630), channel_id=1, source_target_pairs={{0,2},{1,3},{2,0},{3,1},{4,6},{5,7},{6,4},{7,5},{8,10},{9,11},{10,... | collective-permute-start | bytes 393224 | tf_op jit(solution)/shard_map/while/body/eval_jaxpr/ppermute | solution.py:26
  460.2 8.1 collective-permute-start.2
  619.9 16.7 %all-to-all-start = ((bf16[8,2,64,256]{3,2,1,0:T(8,128)(2,1)}), bf16[8,2,64,256]{3,2,1,0:T(8,128)(2,1)S(1)}, u32[]{:S(2)}, u32[]{:S(2)}) async-start(bf16[8,2,64,256]{3,2,1,0:T(8,128)(2,1)} %pad_maximum_fusion.24), calls=%async_computation | async-start | bytes 1048576 | tf_op jit(solution)/shard_map/while/body/eval_jaxpr/all_to_all | solution.py:172
  625.1 54.4 %reduce-scatter.2.cloned.1.call-start = ((), (), s32[]{:S(2)}) async-start(), calls=%async_computation.2 | async-start | bytes 393216 | tf_op jit(solution)/shard_map/while/body/eval_jaxpr/reduce_scatter | solution.py:197
  656.2 10.4 %collective-permute-start = (bf16[2,2,64,256]{3,2,1,0:T(8,128)(2,1)S(1)}, bf16[2,2,64,256]{3,2,1,0:T(8,128)(2,1)S(1)}, u32[]{:S(2)}, u32[]{:S(2)}) collective-permute-start(bf16[2,2,64,256]{3,2,1,0:T(8,128)(2,1)S(1)} %bitcast.629), channel_id=1, source_target_pairs={{0,3},{1,2},{2,1},{3,0},{4,7},{5,6},{6,5},{7,4},{8,11},{9,10},{10,... | collective-permute-start | bytes 393224 | tf_op jit(solution)/shard_map/while/body/eval_jaxpr/ppermute | solution.py:26
  656.9 11.2 %collective-permute-start.1 = (bf16[2,2,64,256]{3,2,1,0:T(8,128)(2,1)S(1)}, bf16[2,2,64,256]{3,2,1,0:T(8,128)(2,1)S(1)}, u32[]{:S(2)}, u32[]{:S(2)}) collective-permute-start(bf16[2,2,64,256]{3,2,1,0:T(8,128)(2,1)S(1)} %bitcast.630), channel_id=1, source_target_pairs={{0,2},{1,3},{2,0},{3,1},{4,6},{5,7},{6,4},{7,5},{8,10},{9,11},{10,... | collective-permute-start | bytes 393224 | tf_op jit(solution)/shard_map/while/body/eval_jaxpr/ppermute | solution.py:26
  820.8 16.6 %all-to-all-start = ((bf16[8,2,64,256]{3,2,1,0:T(8,128)(2,1)}), bf16[8,2,64,256]{3,2,1,0:T(8,128)(2,1)S(1)}, u32[]{:S(2)}, u32[]{:S(2)}) async-start(bf16[8,2,64,256]{3,2,1,0:T(8,128)(2,1)} %pad_maximum_fusion.24), calls=%async_computation | async-start | bytes 1048576 | tf_op jit(solution)/shard_map/while/body/eval_jaxpr/all_to_all | solution.py:172
  826.0 54.4 %reduce-scatter.2.cloned.1.call-start = ((), (), s32[]{:S(2)}) async-start(), calls=%async_computation.2 | async-start | bytes 393216 | tf_op jit(solution)/shard_map/while/body/eval_jaxpr/reduce_scatter | solution.py:197
  857.1 10.5 %collective-permute-start = (bf16[2,2,64,256]{3,2,1,0:T(8,128)(2,1)S(1)}, bf16[2,2,64,256]{3,2,1,0:T(8,128)(2,1)S(1)}, u32[]{:S(2)}, u32[]{:S(2)}) collective-permute-start(bf16[2,2,64,256]{3,2,1,0:T(8,128)(2,1)S(1)} %bitcast.629), channel_id=1, source_target_pairs={{0,3},{1,2},{2,1},{3,0},{4,7},{5,6},{6,5},{7,4},{8,11},{9,10},{10,... | collective-permute-start | bytes 393224 | tf_op jit(solution)/shard_map/while/body/eval_jaxpr/ppermute | solution.py:26
  857.8 11.2 %collective-permute-start.1 = (bf16[2,2,64,256]{3,2,1,0:T(8,128)(2,1)S(1)}, bf16[2,2,64,256]{3,2,1,0:T(8,128)(2,1)S(1)}, u32[]{:S(2)}, u32[]{:S(2)}) collective-permute-start(bf16[2,2,64,256]{3,2,1,0:T(8,128)(2,1)S(1)} %bitcast.630), channel_id=1, source_target_pairs={{0,2},{1,3},{2,0},{3,1},{4,6},{5,7},{6,4},{7,5},{8,10},{9,11},{10,... | collective-permute-start | bytes 393224 | tf_op jit(solution)/shard_map/while/body/eval_jaxpr/ppermute | solution.py:26
  862.0 8.1 collective-permute-start.2
  (94 other events, 826.2 us)
Sparse Core Ops, SparseCore 0:
  67.5 9.3 reduce-scatter.1
  269.2 8.4 reduce-scatter.1
  470.1 8.4 reduce-scatter.1
  671.0 8.4 reduce-scatter.1
  871.9 8.4 reduce-scatter.1
